TPU v7x, 256 devices: a whole 4x4x8 slice. The times are simulated.
256 devices in a mesh: px: 16 (over y, z_hi), py: 16 (over x, z_lo, core).
Axes of the slice: x: 4, y: 4, z: 8 (z_hi: 4, z_lo: 2; z = z_hi * 2 + z_lo), core: 2. Of those that a mesh axis runs over, the one named last changes fastest.
Arguments:
- slab_start: int32 [1], replicated, may hold values from 0 to 96
- fixed_mask: int32 [128, 128, 128], P('px', 'py'), may hold values 0 or 1
- background: float32 [2, 128, 128, 128], P(None, 'px', 'py'), may hold values from -6 to 6
- observed: float32 [2, 128, 128, 128], P(None, 'px', 'py'), may hold values from -6 to 6
- kernel: float32 [2, 2, 256, 256, 256], P(None, None, 'px', 'py'), may hold values from -12 to 12
- frequencies: float32 [3, 128], replicated, may hold values from -48 to 48
- first_weight: bfloat16 [256, 256], replicated, may hold values from -0.375 to 0.375
- second_weight: bfloat16 [256, 256], replicated, may hold values from -0.375 to 0.375
- output_weight: bfloat16 [256, 2], replicated, may hold values from -0.375 to 0.375
Outputs:
- predicted: float32 [2, 128, 128, 128], P(None, 'px', 'py')
- grad_first: float32 [256, 256], replicated
- grad_second: float32 [256, 256], replicated
- grad_output: float32 [256, 2], replicated
Inputs may be any that keep to these rules, and one draw needn't show every extreme that they name: `fixed_mask`: 1 where a cell outside the slab keeps its background value, 0 where it is empty.
All inputs are finite; a program needn't handle non-finite values. No bound on the sum of `fixed_mask` on one device may be relied on, other than what follows from the above.
Results may differ from a plain program's by a relative error of at most 0.0015.
Values sent between devices are 32-bit elements; how exact they have to be, the bound alone decides.
A program may use at most 64 MiB of HBM per device.

v0:
```python
import jax
import jax.numpy as jnp
from jax import lax
from jax.sharding import PartitionSpec as P

SLAB = 32
FEAT = 256


TWO_PI = 6.283185307179586


def dft_tables(count, length):
    rows = lax.broadcasted_iota(jnp.int32, (count, length), 0)
    columns = lax.broadcasted_iota(jnp.int32, (count, length), 1)
    angle = (rows * columns % length).astype(jnp.float32) * (TWO_PI / length)
    return (jnp.cos(angle), jnp.sin(angle))


def contract(form, values, table):
    return jnp.einsum(form, values, table, precision=lax.Precision.HIGHEST)


def complex_pass(form, real_in, imag_in, cosine, sine, direction):
    real_out = contract(form, real_in, cosine) + direction * contract(form, imag_in, sine)
    imag_out = contract(form, imag_in, cosine) - direction * contract(form, real_in, sine)
    return (real_out, imag_out)


def forward_transform(fields, cosine, sine):
    real_part = contract("fyzj,jk->fyzk", fields, cosine)
    imag_part = -contract("fyzj,jk->fyzk", fields, sine)
    pair = (
        lax.all_to_all(real_part, "px", split_axis=3, concat_axis=1, tiled=True),
        lax.all_to_all(imag_part, "px", split_axis=3, concat_axis=1, tiled=True),
    )
    middle = complex_pass("fjzk,jq->fzkq", pair[0], pair[1], cosine, sine, 1.0)
    pair = (
        lax.all_to_all(middle[0], "py", split_axis=3, concat_axis=1, tiled=True),
        lax.all_to_all(middle[1], "py", split_axis=3, concat_axis=1, tiled=True),
    )
    return complex_pass("fjkq,jr->fkqr", pair[0], pair[1], cosine, sine, 1.0)


def inverse_transform(real_part, imag_part, cosine, sine):
    real_z, imag_z = complex_pass("fkqr,jr->fkqj", real_part, imag_part, cosine, sine, -1.0)
    pair = (
        lax.all_to_all(real_z, "py", split_axis=3, concat_axis=2, tiled=True),
        lax.all_to_all(imag_z, "py", split_axis=3, concat_axis=2, tiled=True),
    )
    middle = complex_pass("fkqz,jq->fkzj", pair[0], pair[1], cosine, sine, -1.0)
    pair = (
        lax.all_to_all(middle[0], "px", split_axis=3, concat_axis=1, tiled=True),
        lax.all_to_all(middle[1], "px", split_axis=3, concat_axis=1, tiled=True),
    )
    spatial = contract("fkzy,jk->fyzj", pair[0], cosine) - contract("fkzy,jk->fyzj", pair[1], sine)
    length = cosine.shape[1]
    return spatial * (1.0 / float(length) ** 3)


def round_trip(fields, kernel, direction, cosine, sine):
    real_part, imag_part = forward_transform(fields, cosine, sine)
    kernel_real = kernel[:, 0]
    kernel_imag = kernel[:, 1]
    product_real = kernel_real * real_part - direction * kernel_imag * imag_part
    product_imag = kernel_real * imag_part + direction * kernel_imag * real_part
    return inverse_transform(product_real, product_imag, cosine, sine)


def apply_operator(fields, kernel, direction, cosine, sine):
    pieces = [
        round_trip(
            fields[field_index : field_index + 1],
            kernel[field_index : field_index + 1],
            direction,
            cosine,
            sine,
        )
        for field_index in range(2)
    ]
    return jnp.concatenate(pieces, 0)


def on_device(
    slab_start,
    fixed_mask,
    background,
    observed,
    kernel,
    frequencies,
    first_weight,
    second_weight,
    output_weight,
):
    y_count, z_count, grid = fixed_mask.shape
    length = kernel.shape[4]
    first_plane = slab_start[0]
    y_coord = (lax.axis_index("px") * y_count + jnp.arange(y_count, dtype=jnp.int32)).astype(
        jnp.float32
    ) / grid
    z_coord = (lax.axis_index("py") * z_count + jnp.arange(z_count, dtype=jnp.int32)).astype(
        jnp.float32
    ) / grid
    x_coord = (first_plane + jnp.arange(SLAB, dtype=jnp.int32)).astype(jnp.float32) / grid
    phase = (
        x_coord[None, None, :, None] * frequencies[0]
        + y_coord[:, None, None, None] * frequencies[1]
        + z_coord[None, :, None, None] * frequencies[2]
    ) * TWO_PI
    features = (
        jnp.concatenate([jnp.sin(phase), jnp.cos(phase)], -1).astype(jnp.bfloat16).reshape(-1, FEAT)
    )
    hidden_one = jnp.tanh(
        jnp.dot(features, first_weight, preferred_element_type=jnp.float32)
    ).astype(jnp.bfloat16)
    hidden_two = jnp.tanh(
        jnp.dot(hidden_one, second_weight, preferred_element_type=jnp.float32)
    ).astype(jnp.bfloat16)
    network = jnp.einsum("rh,hc->cr", hidden_two, output_weight, preferred_element_type=jnp.float32)
    slab_values = network.reshape(2, y_count, z_count, SLAB)
    zero = jnp.zeros((), jnp.int32)
    placed = lax.dynamic_update_slice(
        jnp.zeros((2, y_count, z_count, grid), jnp.float32),
        slab_values,
        (zero, zero, zero, first_plane),
    )
    plane_index = jnp.arange(grid, dtype=jnp.int32)
    inside = (plane_index >= first_plane) & (plane_index < first_plane + SLAB)
    fields = jnp.where(inside, placed, fixed_mask.astype(jnp.float32) * background)
    cosine, sine = dft_tables(grid, length)
    predicted = apply_operator(fields, kernel, 1.0, cosine, sine)
    residual = (predicted - observed) / grid
    adjoint = apply_operator(residual, kernel, -1.0, cosine, sine)
    cotangent = (
        lax.dynamic_slice(adjoint, (zero, zero, zero, first_plane), (2, y_count, z_count, SLAB))
        .reshape(2, -1)
        .astype(jnp.bfloat16)
    )
    grad_output = jnp.einsum("rh,cr->hc", hidden_two, cotangent, preferred_element_type=jnp.float32)
    back_two = jnp.einsum("cr,hc->rh", cotangent, output_weight, preferred_element_type=jnp.float32)
    two_values = hidden_two.astype(jnp.float32)
    delta_two = (back_two * (1.0 - two_values * two_values)).astype(jnp.bfloat16)
    grad_second = jnp.einsum("rh,rk->hk", hidden_one, delta_two, preferred_element_type=jnp.float32)
    back_one = jnp.einsum("rk,hk->rh", delta_two, second_weight, preferred_element_type=jnp.float32)
    one_values = hidden_one.astype(jnp.float32)
    delta_one = (back_one * (1.0 - one_values * one_values)).astype(jnp.bfloat16)
    grad_first = jnp.einsum("rf,rh->fh", features, delta_one, preferred_element_type=jnp.float32)
    grad_first, grad_second, grad_output = lax.psum(
        (grad_first, grad_second, grad_output), ("px", "py")
    )
    return (predicted, grad_first, grad_second, grad_output)


def solution(mesh):
    return jax.shard_map(
        on_device,
        mesh=mesh,
        in_specs=(
            P(),
            P("px", "py", None),
            P(None, "px", "py", None),
            P(None, "px", "py", None),
            P(None, None, "px", "py", None),
            P(),
            P(),
            P(),
            P(),
        ),
        out_specs=(P(None, "px", "py", None), P(), P(), P()),
        check_vma=False,
    )
```

profile of v0, /device:TPU:1, one launch (start us, length us, event | category | flops | bytes accessed | tf_op | source)
XLA Modules:
  0.0 822.2 jit_solution(3476414815314963687)
XLA Ops:
  9.7 3.8 sine_convert_fusion
  16.0 2.5 dynamic_update_slice.3
  20.7 11.7 %all-to-all-start = ((f32[16,1,1024]{2,1,0:T(1,128)}), f32[16,1,1024]{2,1,0:T(1,128)S(1)}, u32[]{:S(2)}, u32[]{:S(2)}) async-start(f32[16,1,1024]{2,1,0:T(1,128)} %reshape.639), calls=%async_computation | async-start | bytes 131072 | tf_op jit(solution)/shard_map/all_to_all | solution.py:34
  37.0 4.5 all-to-all-done
  41.5 4.6 all-to-all-start.8
  52.7 2.6 all-to-all-done.8
  55.2 6.5 all-to-all-start.1
  67.6 3.2 all-to-all-done.1
  70.8 5.8 all-to-all-start.9
  85.7 8.5 %all-to-all-start.3 = ((f32[16,1,2048]{2,1,0:T(1,128)}), f32[16,1,2048]{2,1,0:T(1,128)S(1)}, u32[]{:S(2)}, u32[]{:S(2)}) async-start(f32[16,1,2048]{2,1,0:T(1,128)} %reshape.645), calls=%async_computation.3 | async-start | bytes 262144 | tf_op jit(solution)/shard_map/all_to_all | solution.py:40
  94.2 2.4 fusion.28
  103.5 5.7 all-to-all-start.2
  118.9 5.7 all-to-all-start.11
  133.0 5.9 all-to-all-start.10
  145.6 2.5 reduce.6
  155.0 2.8 fusion.58
  164.4 5.7 all-to-all-start.12
  176.2 4.8 all-to-all-start.13
  181.1 2.5 fusion.18
  186.0 2.5 fusion.20
  194.8 5.7 all-to-all-start.5
  207.5 6.4 all-to-all-start.4
  220.6 7.4 all-to-all-start.14
  235.4 2.1 all-to-all-done.14
  237.5 7.0 all-to-all-start.15
  245.3 8.4 %all-to-all-done.15 = f32[16,1,1024]{2,1,0:T(1,128)S(1)} async-done(((f32[16,1,1024]{2,1,0:T(1,128)}), f32[16,1,1024]{2,1,0:T(1,128)S(1)}, u32[]{:S(2)}, u32[]{:S(2)}) %all-to-all-start.15) | async-done | bytes 65568 | tf_op jit(solution)/shard_map/all_to_all | solution.py:54
  253.7 3.5 all-to-all-start.7
  262.0 4.4 all-to-all-done.7
  266.4 4.8 all-to-all-start.6
  273.5 7.0 all-to-all-done.6
  287.8 3.5 all-to-all-start.24
  295.2 5.4 all-to-all-done.24
  300.6 3.6 all-to-all-start.25
  310.9 2.5 all-to-all-done.25
  313.4 6.7 all-to-all-start.16
  329.3 8.2 all-to-all-start.17
  344.2 2.6 all-to-all-done.17
  347.3 12.0 %all-to-all-start.27 = ((f32[16,1,2048]{2,1,0:T(1,128)}), f32[16,1,2048]{2,1,0:T(1,128)S(1)}, u32[]{:S(2)}, u32[]{:S(2)}) async-start(f32[16,1,2048]{2,1,0:T(1,128)} %reshape.659), calls=%async_computation.27 | async-start | bytes 262144 | tf_op jit(solution)/shard_map/all_to_all | solution.py:40
  370.2 6.3 all-to-all-start.26
  376.5 2.3 fusion.23
  388.4 5.7 all-to-all-start.19
  394.1 1.9 reduce.22
  401.8 6.0 all-to-all-start.18
  407.8 2.5 reduce.18
  417.7 2.5 reduce.19
  426.3 2.9 fusion.60
  435.5 6.0 all-to-all-start.28
  447.5 4.9 all-to-all-start.29
  452.5 2.5 fusion.10
  457.4 2.5 fusion.12
  466.2 5.7 all-to-all-start.21
  478.9 6.4 all-to-all-start.20
  492.0 5.8 all-to-all-start.30
  497.8 1.9 reduce.29
  505.2 2.1 all-to-all-done.30
  507.3 7.0 all-to-all-start.31
  515.1 8.4 %all-to-all-done.31 = f32[16,1,1024]{2,1,0:T(1,128)S(1)} async-done(((f32[16,1,1024]{2,1,0:T(1,128)}), f32[16,1,1024]{2,1,0:T(1,128)S(1)}, u32[]{:S(2)}, u32[]{:S(2)}) %all-to-all-start.31) | async-done | bytes 65568 | tf_op jit(solution)/shard_map/all_to_all | solution.py:54
  523.5 3.5 all-to-all-start.23
  531.8 4.4 all-to-all-done.23
  536.2 4.6 all-to-all-start.22
  543.3 6.7 all-to-all-done.22
  554.6 2.8 fusion.4
  559.5 77.7 %psum.23 = f32[256,2]{0,1:T(2,128)} all-reduce(f32[256,2]{0,1:T(2,128)S(1)} %fusion.576), channel_id=1, replica_groups=mesh['px'=16,'py'=16] {'px','py'}, use_global_device_ids=true, to_apply=%region_2.3 | all-reduce | flops 512 | bytes 4096 | tf_op jit(solution)/shard_map/psum | solution.py:148
  637.2 174.6 %all-reduce.3.cloned.1.call-done = (f32[256,256]{1,0:T(8,128)}, f32[256,256]{1,0:T(8,128)}) async-done(((f32[256,256]{1,0:T(8,128)}, f32[256,256]{1,0:T(8,128)}), (f32[256,256]{1,0:T(8,128)}, f32[256,256]{1,0:T(8,128)})) %all-reduce.3.cloned.1.call-update) | async-done | bytes 524304 | tf_op jit(solution)/shard_map/psum | solution.py:148
  (438 shorter events, 252.0 us)
Async XLA Ops:
  7.2 7.6 copy-start
  7.2 7.1 copy-start.54
  20.7 20.8 %all-to-all-start = ((f32[16,1,1024]{2,1,0:T(1,128)}), f32[16,1,1024]{2,1,0:T(1,128)S(1)}, u32[]{:S(2)}, u32[]{:S(2)}) async-start(f32[16,1,1024]{2,1,0:T(1,128)} %reshape.639), calls=%async_computation | async-start | bytes 131072 | tf_op jit(solution)/shard_map/all_to_all | solution.py:34
  41.5 13.7 %all-to-all-start.8 = ((f32[16,1,1024]{2,1,0:T(1,128)}), f32[16,1,1024]{2,1,0:T(1,128)S(1)}, u32[]{:S(2)}, u32[]{:S(2)}) async-start(f32[16,1,1024]{2,1,0:T(1,128)} %reshape.623), calls=%async_computation.8 | async-start | bytes 131072 | tf_op jit(solution)/shard_map/all_to_all | solution.py:34
  52.7 13.5 %copy-start.44 = (f32[128,8,16]{0,2,1:T(8,128)}, f32[128,8,16]{0,2,1:T(8,128)S(1)}, u32[]{:S(2)}) copy-start(f32[128,8,16]{0,2,1:T(8,128)S(1)} %copy.259) | copy-start | bytes 196612
  55.2 15.6 %all-to-all-start.1 = ((f32[16,1,1024]{2,1,0:T(1,128)}), f32[16,1,1024]{2,1,0:T(1,128)S(1)}, u32[]{:S(2)}, u32[]{:S(2)}) async-start(f32[16,1,1024]{2,1,0:T(1,128)} %reshape.641), calls=%async_computation.1 | async-start | bytes 131072 | tf_op jit(solution)/shard_map/all_to_all | solution.py:35
  70.8 14.9 %all-to-all-start.9 = ((f32[16,1,1024]{2,1,0:T(1,128)}), f32[16,1,1024]{2,1,0:T(1,128)S(1)}, u32[]{:S(2)}, u32[]{:S(2)}) async-start(f32[16,1,1024]{2,1,0:T(1,128)} %reshape.625), calls=%async_computation.9 | async-start | bytes 131072 | tf_op jit(solution)/shard_map/all_to_all | solution.py:35
  85.7 17.8 %all-to-all-start.3 = ((f32[16,1,2048]{2,1,0:T(1,128)}), f32[16,1,2048]{2,1,0:T(1,128)S(1)}, u32[]{:S(2)}, u32[]{:S(2)}) async-start(f32[16,1,2048]{2,1,0:T(1,128)} %reshape.645), calls=%async_computation.3 | async-start | bytes 262144 | tf_op jit(solution)/shard_map/all_to_all | solution.py:40
  101.5 7.8 copy-start.42
  102.7 6.5 copy-start.50
  103.5 15.4 %all-to-all-start.2 = ((f32[16,1,2048]{2,1,0:T(1,128)}), f32[16,1,2048]{2,1,0:T(1,128)}, u32[]{:S(2)}, u32[]{:S(2)}) async-start(f32[16,1,2048]{2,1,0:T(1,128)} %reshape.643), calls=%async_computation.2 | async-start | bytes 262144 | tf_op jit(solution)/shard_map/all_to_all | solution.py:39
  118.9 7.3 copy-start.6
  118.9 14.0 %all-to-all-start.11 = ((f32[16,1,2048]{2,1,0:T(1,128)}), f32[16,1,2048]{2,1,0:T(1,128)S(1)}, u32[]{:S(2)}, u32[]{:S(2)}) async-start(f32[16,1,2048]{2,1,0:T(1,128)} %reshape.629), calls=%async_computation.11 | async-start | bytes 262144 | tf_op jit(solution)/shard_map/all_to_all | solution.py:40
  131.4 7.5 copy-start.2
  133.0 12.6 %all-to-all-start.10 = ((f32[16,1,2048]{2,1,0:T(1,128)}), f32[16,1,2048]{2,1,0:T(1,128)}, u32[]{:S(2)}, u32[]{:S(2)}) async-start(f32[16,1,2048]{2,1,0:T(1,128)} %reshape.627), calls=%async_computation.10 | async-start | bytes 262144 | tf_op jit(solution)/shard_map/all_to_all | solution.py:39
  141.5 3.2 copy-start.7
  141.5 3.2 copy-start.24
  150.7 3.4 copy-start.11
  157.9 3.9 copy-start.19
  157.9 3.9 copy-start.21
  164.4 11.8 %all-to-all-start.12 = ((f32[16,1,2048]{2,1,0:T(1,128)}), f32[16,1,2048]{2,1,0:T(1,128)S(1)}, u32[]{:S(2)}, u32[]{:S(2)}) async-start(f32[16,1,2048]{2,1,0:T(1,128)} %reshape.633), calls=%async_computation.12 | async-start | bytes 262144 | tf_op jit(solution)/shard_map/all_to_all | solution.py:48
  176.2 9.7 %copy-start.16 = (f32[16,1,2048]{2,1,0:T(1,128)}, f32[16,1,2048]{2,1,0:T(1,128)S(1)}, u32[]{:S(2)}) copy-start(f32[16,1,2048]{2,1,0:T(1,128)S(1)} %all-to-all-done.12) | copy-start | bytes 393220
  176.2 17.9 %all-to-all-start.13 = ((f32[16,1,2048]{2,1,0:T(1,128)}), f32[16,1,2048]{2,1,0:T(1,128)S(1)}, u32[]{:S(2)}, u32[]{:S(2)}) async-start(f32[16,1,2048]{2,1,0:T(1,128)} %reshape.631), calls=%async_computation.13 | async-start | bytes 262144 | tf_op jit(solution)/shard_map/all_to_all | solution.py:49
  194.1 6.4 copy-start.32
  194.8 12.6 %all-to-all-start.5 = ((f32[16,1,2048]{2,1,0:T(1,128)}), f32[16,1,2048]{2,1,0:T(1,128)S(1)}, u32[]{:S(2)}, u32[]{:S(2)}) async-start(f32[16,1,2048]{2,1,0:T(1,128)} %reshape.647), calls=%async_computation.5 | async-start | bytes 262144 | tf_op jit(solution)/shard_map/all_to_all | solution.py:49
  204.7 9.2 %copy-start.33 = (f32[16,256,8]{1,2,0:T(8,128)S(1)}, f32[16,256,8]{1,2,0:T(8,128)}, u32[]{:S(2)}) copy-start(f32[16,256,8]{1,2,0:T(8,128)} %copy-done.32) | copy-start | bytes 393220
  207.5 8.4 %copy-start.38 = (f32[16,256,8]{1,2,0:T(8,128)S(1)}, f32[16,256,8]{1,2,0:T(8,128)}, u32[]{:S(2)}) copy-start(f32[16,256,8]{1,2,0:T(8,128)} %reshape.576) | copy-start | bytes 393220
  207.5 8.4 %copy-start.56 = (f32[16,8,128]{2,1,0:T(8,128)S(1)}, f32[16,8,128]{2,1,0:T(8,128)}, u32[]{:S(2)}) copy-start(f32[16,8,128]{2,1,0:T(8,128)} %convolution_multiply_fusion.14) | copy-start | bytes 196612
  207.5 13.1 %all-to-all-start.4 = ((f32[16,1,2048]{2,1,0:T(1,128)}), f32[16,1,2048]{2,1,0:T(1,128)}, u32[]{:S(2)}, u32[]{:S(2)}) async-start(f32[16,1,2048]{2,1,0:T(1,128)} %reshape.649), calls=%async_computation.4 | async-start | bytes 262144 | tf_op jit(solution)/shard_map/all_to_all | solution.py:48
  220.6 16.9 %all-to-all-start.14 = ((f32[16,1,1024]{2,1,0:T(1,128)}), f32[16,1,1024]{2,1,0:T(1,128)S(1)}, u32[]{:S(2)}, u32[]{:S(2)}) async-start(f32[16,1,1024]{2,1,0:T(1,128)} %reshape.635), calls=%async_computation.14 | async-start | bytes 131072 | tf_op jit(solution)/shard_map/all_to_all | solution.py:53
  234.3 22.9 %copy-start.36 = (f32[16,256,8]{1,2,0:T(8,128)S(1)}, f32[16,256,8]{1,2,0:T(8,128)}, u32[]{:S(2)}) copy-start(f32[16,256,8]{1,2,0:T(8,128)} %reshape.566) | copy-start | bytes 393220
  237.5 16.2 %all-to-all-start.15 = ((f32[16,1,1024]{2,1,0:T(1,128)}), f32[16,1,1024]{2,1,0:T(1,128)S(1)}, u32[]{:S(2)}, u32[]{:S(2)}) async-start(f32[16,1,1024]{2,1,0:T(1,128)} %reshape.637), calls=%async_computation.15 | async-start | bytes 131072 | tf_op jit(solution)/shard_map/all_to_all | solution.py:54
  253.7 12.7 %all-to-all-start.7 = ((f32[16,1,1024]{2,1,0:T(1,128)}), f32[16,1,1024]{2,1,0:T(1,128)S(1)}, u32[]{:S(2)}, u32[]{:S(2)}) async-start(f32[16,1,1024]{2,1,0:T(1,128)} %reshape.653), calls=%async_computation.7 | async-start | bytes 131072 | tf_op jit(solution)/shard_map/all_to_all | solution.py:54
  266.4 14.0 %all-to-all-start.6 = ((f32[16,1,1024]{2,1,0:T(1,128)}), f32[16,1,1024]{2,1,0:T(1,128)S(1)}, u32[]{:S(2)}, u32[]{:S(2)}) async-start(f32[16,1,1024]{2,1,0:T(1,128)} %reshape.651), calls=%async_computation.6 | async-start | bytes 131072 | tf_op jit(solution)/shard_map/all_to_all | solution.py:53
  287.8 12.7 %all-to-all-start.24 = ((f32[16,1,1024]{2,1,0:T(1,128)}), f32[16,1,1024]{2,1,0:T(1,128)S(1)}, u32[]{:S(2)}, u32[]{:S(2)}) async-start(f32[16,1,1024]{2,1,0:T(1,128)} %reshape.657), calls=%async_computation.24 | async-start | bytes 131072 | tf_op jit(solution)/shard_map/all_to_all | solution.py:34
  300.6 12.9 %all-to-all-start.25 = ((f32[16,1,1024]{2,1,0:T(1,128)}), f32[16,1,1024]{2,1,0:T(1,128)S(1)}, u32[]{:S(2)}, u32[]{:S(2)}) async-start(f32[16,1,1024]{2,1,0:T(1,128)} %reshape.655), calls=%async_computation.25 | async-start | bytes 131072 | tf_op jit(solution)/shard_map/all_to_all | solution.py:35
  313.4 15.9 %all-to-all-start.16 = ((f32[16,1,1024]{2,1,0:T(1,128)}), f32[16,1,1024]{2,1,0:T(1,128)S(1)}, u32[]{:S(2)}, u32[]{:S(2)}) async-start(f32[16,1,1024]{2,1,0:T(1,128)} %reshape.673), calls=%async_computation.16 | async-start | bytes 131072 | tf_op jit(solution)/shard_map/all_to_all | solution.py:34
  329.3 17.4 %all-to-all-start.17 = ((f32[16,1,1024]{2,1,0:T(1,128)}), f32[16,1,1024]{2,1,0:T(1,128)S(1)}, u32[]{:S(2)}, u32[]{:S(2)}) async-start(f32[16,1,1024]{2,1,0:T(1,128)} %reshape.671), calls=%async_computation.17 | async-start | bytes 131072 | tf_op jit(solution)/shard_map/all_to_all | solution.py:35
  338.9 3.8 copy-start.47
  341.3 18.0 %copy-start.43 = (f32[128,8,16]{0,2,1:T(8,128)}, f32[128,8,16]{0,2,1:T(8,128)S(1)}, u32[]{:S(2)}) copy-start(f32[128,8,16]{0,2,1:T(8,128)S(1)} %copy.317) | copy-start | bytes 196612
  347.3 22.9 %all-to-all-start.27 = ((f32[16,1,2048]{2,1,0:T(1,128)}), f32[16,1,2048]{2,1,0:T(1,128)S(1)}, u32[]{:S(2)}, u32[]{:S(2)}) async-start(f32[16,1,2048]{2,1,0:T(1,128)} %reshape.659), calls=%async_computation.27 | async-start | bytes 262144 | tf_op jit(solution)/shard_map/all_to_all | solution.py:40
  370.2 18.2 %all-to-all-start.26 = ((f32[16,1,2048]{2,1,0:T(1,128)}), f32[16,1,2048]{2,1,0:T(1,128)}, u32[]{:S(2)}, u32[]{:S(2)}) async-start(f32[16,1,2048]{2,1,0:T(1,128)} %reshape.661), calls=%async_computation.26 | async-start | bytes 262144 | tf_op jit(solution)/shard_map/all_to_all | solution.py:39
  386.8 7.3 copy-start.4
  388.4 13.4 %all-to-all-start.19 = ((f32[16,1,2048]{2,1,0:T(1,128)}), f32[16,1,2048]{2,1,0:T(1,128)}, u32[]{:S(2)}, u32[]{:S(2)}) async-start(f32[16,1,2048]{2,1,0:T(1,128)} %reshape.675), calls=%async_computation.19 | async-start | bytes 262144 | tf_op jit(solution)/shard_map/all_to_all | solution.py:40
  401.8 16.0 %all-to-all-start.18 = ((f32[16,1,2048]{2,1,0:T(1,128)}), f32[16,1,2048]{2,1,0:T(1,128)}, u32[]{:S(2)}, u32[]{:S(2)}) async-start(f32[16,1,2048]{2,1,0:T(1,128)} %reshape.677), calls=%async_computation.18 | async-start | bytes 262144 | tf_op jit(solution)/shard_map/all_to_all | solution.py:39
  422.9 3.4 copy-start.1
  422.9 3.4 copy-start.9
  429.1 3.9 copy-start.20
  429.1 3.9 copy-start.22
  435.5 12.0 %all-to-all-start.28 = ((f32[16,1,2048]{2,1,0:T(1,128)}), f32[16,1,2048]{2,1,0:T(1,128)S(1)}, u32[]{:S(2)}, u32[]{:S(2)}) async-start(f32[16,1,2048]{2,1,0:T(1,128)} %reshape.665), calls=%async_computation.28 | async-start | bytes 262144 | tf_op jit(solution)/shard_map/all_to_all | solution.py:48
  447.5 9.8 %copy-start.17 = (f32[16,1,2048]{2,1,0:T(1,128)}, f32[16,1,2048]{2,1,0:T(1,128)S(1)}, u32[]{:S(2)}) copy-start(f32[16,1,2048]{2,1,0:T(1,128)S(1)} %all-to-all-done.28) | copy-start | bytes 393220
  447.5 18.0 %all-to-all-start.29 = ((f32[16,1,2048]{2,1,0:T(1,128)}), f32[16,1,2048]{2,1,0:T(1,128)S(1)}, u32[]{:S(2)}, u32[]{:S(2)}) async-start(f32[16,1,2048]{2,1,0:T(1,128)} %reshape.663), calls=%async_computation.29 | async-start | bytes 262144 | tf_op jit(solution)/shard_map/all_to_all | solution.py:49
  465.5 6.4 copy-start.34
  466.2 12.7 %all-to-all-start.21 = ((f32[16,1,2048]{2,1,0:T(1,128)}), f32[16,1,2048]{2,1,0:T(1,128)S(1)}, u32[]{:S(2)}, u32[]{:S(2)}) async-start(f32[16,1,2048]{2,1,0:T(1,128)} %reshape.679), calls=%async_computation.21 | async-start | bytes 262144 | tf_op jit(solution)/shard_map/all_to_all | solution.py:49
  476.1 9.2 %copy-start.35 = (f32[16,256,8]{1,2,0:T(8,128)S(1)}, f32[16,256,8]{1,2,0:T(8,128)}, u32[]{:S(2)}) copy-start(f32[16,256,8]{1,2,0:T(8,128)} %copy-done.34) | copy-start | bytes 393220
  478.9 8.3 %copy-start.39 = (f32[16,256,8]{1,2,0:T(8,128)S(1)}, f32[16,256,8]{1,2,0:T(8,128)}, u32[]{:S(2)}) copy-start(f32[16,256,8]{1,2,0:T(8,128)} %reshape.594) | copy-start | bytes 393220
  478.9 8.3 %copy-start.57 = (f32[16,8,128]{2,1,0:T(8,128)S(1)}, f32[16,8,128]{2,1,0:T(8,128)}, u32[]{:S(2)}) copy-start(f32[16,8,128]{2,1,0:T(8,128)} %convolution_multiply_fusion.10) | copy-start | bytes 196612
  478.9 13.1 %all-to-all-start.20 = ((f32[16,1,2048]{2,1,0:T(1,128)}), f32[16,1,2048]{2,1,0:T(1,128)}, u32[]{:S(2)}, u32[]{:S(2)}) async-start(f32[16,1,2048]{2,1,0:T(1,128)} %reshape.681), calls=%async_computation.20 | async-start | bytes 262144 | tf_op jit(solution)/shard_map/all_to_all | solution.py:48
  492.0 15.3 %all-to-all-start.30 = ((f32[16,1,1024]{2,1,0:T(1,128)}), f32[16,1,1024]{2,1,0:T(1,128)S(1)}, u32[]{:S(2)}, u32[]{:S(2)}) async-start(f32[16,1,1024]{2,1,0:T(1,128)} %reshape.667), calls=%async_computation.30 | async-start | bytes 131072 | tf_op jit(solution)/shard_map/all_to_all | solution.py:53
  504.1 22.9 %copy-start.37 = (f32[16,256,8]{1,2,0:T(8,128)S(1)}, f32[16,256,8]{1,2,0:T(8,128)}, u32[]{:S(2)}) copy-start(f32[16,256,8]{1,2,0:T(8,128)} %reshape.584) | copy-start | bytes 393220
  507.3 16.2 %all-to-all-start.31 = ((f32[16,1,1024]{2,1,0:T(1,128)}), f32[16,1,1024]{2,1,0:T(1,128)S(1)}, u32[]{:S(2)}, u32[]{:S(2)}) async-start(f32[16,1,1024]{2,1,0:T(1,128)} %reshape.669), calls=%async_computation.31 | async-start | bytes 131072 | tf_op jit(solution)/shard_map/all_to_all | solution.py:54
  523.5 12.7 %all-to-all-start.23 = ((f32[16,1,1024]{2,1,0:T(1,128)}), f32[16,1,1024]{2,1,0:T(1,128)S(1)}, u32[]{:S(2)}, u32[]{:S(2)}) async-start(f32[16,1,1024]{2,1,0:T(1,128)} %reshape.685), calls=%async_computation.23 | async-start | bytes 131072 | tf_op jit(solution)/shard_map/all_to_all | solution.py:54
  536.2 13.8 %all-to-all-start.22 = ((f32[16,1,1024]{2,1,0:T(1,128)}), f32[16,1,1024]{2,1,0:T(1,128)S(1)}, u32[]{:S(2)}, u32[]{:S(2)}) async-start(f32[16,1,1024]{2,1,0:T(1,128)} %reshape.683), calls=%async_computation.22 | async-start | bytes 131072 | tf_op jit(solution)/shard_map/all_to_all | solution.py:53
  540.9 270.9 %all-reduce.3.cloned.1.call-start = ((), (), s32[]{:S(2)}) async-start(), calls=%async_computation.32 | async-start | bytes 1048576 | tf_op jit(solution)/shard_map/psum | solution.py:148
  (27 other events, 55.2 us)
Sparse Core Ops, SparseCore 0:
  558.7 253.0 all-reduce.2
where the time goes:
time: 836 us; the launch traced here: 822 us
  waiting for transfers between devices  242 us (29%)
  starting transfers between devices  196 us (23%)
  local copies, waits for them, and re-layouts  137 us (16%)
  matrix products  105 us (13%)
  blocking collectives  77.7 us (9%)
  other arithmetic  46.3 us (6%)
  between operations  17.1 us (2%)
    psum x1, waiting for transfers between devices, on_device(): lax.psum((grad_first, grad_second, grad_output), ('px', 'py'))  175 us
    dot_general x72, matrix products, contract(): return jnp.einsum(form, values, table, precision=lax.Precision.HIGHEST)  93.3 us
    psum x1, blocking collectives, on_device(): lax.psum((grad_first, grad_second, grad_output), ('px', 'py'))  77.7 us
    unnamed x191, local copies, waits for them, and re-layouts  57.4 us
    all_to_all x4, starting transfers between devices, forward_transform(): lax.all_to_all(middle[1], 'py', split_axis=3, concat_axis=1, tiled=True)  31.9 us
    another operation x25, local copies, waits for them, and re-layouts  31.3 us
    all_to_all x4, starting transfers between devices, forward_transform(): lax.all_to_all(real_part, 'px', split_axis=3, concat_axis=1, tiled=True)  26.6 us
    all_to_all x4, waiting for transfers between devices, inverse_transform(): lax.all_to_all(middle[1], 'px', split_axis=3, concat_axis=1, tiled=True)  25.6 us
  transfers between devices with their start and end apart: 33, of which 19 were waited for; matrix products, arithmetic and copies ran while one was open for 26% of the time, Pallas kernels for 0%

commit v1 on v0

v1 whole, which is shorter than its diff:
```python
import jax
import jax.numpy as jnp
from jax import lax
from jax.sharding import PartitionSpec as P

SLAB = 32
FEAT = 256
TWO_PI = 6.283185307179586
PRECISION = lax.Precision.HIGH


def angles(count_in, count_out, length):
    rows = lax.broadcasted_iota(jnp.int32, (count_in, count_out), 0)
    columns = lax.broadcasted_iota(jnp.int32, (count_in, count_out), 1)
    angle = (rows * columns % length).astype(jnp.float32) * (TWO_PI / length)
    return jnp.cos(angle), jnp.sin(angle)


def complex_table(count_in, count_out, length, sign):
    cosine, sine = angles(count_in, count_out, length)
    top = jnp.stack([cosine, sign * sine], 1)
    bottom = jnp.stack([-sign * sine, cosine], 1)
    return jnp.stack([top, bottom], 0)


def contract(form, values, table):
    return jnp.einsum(form, values, table, precision=PRECISION)


def round_trip(fields, kernel_real, kernel_imag, direction, tables, ranks):
    x_forward, y_forward, z_forward, z_inverse, y_inverse, x_inverse = tables
    px_size, py_size = ranks
    spectrum = contract("fyzx,xckl->kcfyzl", fields, x_forward)
    spectrum = lax.all_to_all(spectrum, "px", 0, 0, tiled=True)
    spectrum = contract("scfyzl,csydmq->mdfzlq", spectrum, y_forward)
    spectrum = lax.all_to_all(spectrum, "py", 0, 0, tiled=True)
    spectrum = contract("sdfzlq,dszek->eflqk", spectrum, z_forward)
    real_part = spectrum[0]
    imag_part = spectrum[1]
    product_real = kernel_real * real_part - direction * (kernel_imag * imag_part)
    product_imag = kernel_real * imag_part + direction * (kernel_imag * real_part)
    product = jnp.stack([product_real, product_imag], 0)
    back = contract("eflqk,ekgmz->mgflqz", product, z_inverse)
    back = lax.all_to_all(back, "py", 0, 0, tiled=True)
    back = contract("sgflqz,gsqhmy->mhfyzl", back, y_inverse)
    back = lax.all_to_all(back, "px", 0, 0, tiled=True)
    return contract("shfyzl,hslx->fyzx", back, x_inverse)


def gradient_sum(parts):
    flat = jnp.concatenate([part.reshape(-1) for part in parts])
    count = flat.shape[0]
    devices = lax.axis_size("px") * lax.axis_size("py")
    padded = jnp.pad(flat, (0, (-count) % devices))
    share = padded.shape[0] // devices
    summed = lax.all_to_all(padded.reshape(devices, share), ("px", "py"), 0, 0, tiled=True)
    summed = summed.sum(0)
    gathered = jnp.broadcast_to(summed[None], (devices, share))
    gathered = lax.all_to_all(gathered, ("px", "py"), 0, 0, tiled=True).reshape(-1)
    result = []
    offset = 0
    for part in parts:
        result.append(gathered[offset : offset + part.size].reshape(part.shape))
        offset += part.size
    return tuple(result)


def on_device(
    slab_start,
    fixed_mask,
    background,
    observed,
    kernel,
    frequencies,
    first_weight,
    second_weight,
    output_weight,
):
    y_count, z_count, grid = fixed_mask.shape
    length = kernel.shape[4]
    px_size = lax.axis_size("px")
    py_size = lax.axis_size("py")
    kx_count = kernel.shape[2]
    ky_count = kernel.shape[3]
    first_plane = slab_start[0]
    y_coord = (lax.axis_index("px") * y_count + jnp.arange(y_count, dtype=jnp.int32)).astype(
        jnp.float32
    ) / grid
    z_coord = (lax.axis_index("py") * z_count + jnp.arange(z_count, dtype=jnp.int32)).astype(
        jnp.float32
    ) / grid
    x_coord = (first_plane + jnp.arange(SLAB, dtype=jnp.int32)).astype(jnp.float32) / grid
    phase = (
        x_coord[None, None, :, None] * frequencies[0]
        + y_coord[:, None, None, None] * frequencies[1]
        + z_coord[None, :, None, None] * frequencies[2]
    ) * TWO_PI
    features = (
        jnp.concatenate([jnp.sin(phase), jnp.cos(phase)], -1).astype(jnp.bfloat16).reshape(-1, FEAT)
    )
    hidden_one = jnp.tanh(
        jnp.dot(features, first_weight, preferred_element_type=jnp.float32)
    ).astype(jnp.bfloat16)
    hidden_two = jnp.tanh(
        jnp.dot(hidden_one, second_weight, preferred_element_type=jnp.float32)
    ).astype(jnp.bfloat16)
    network = jnp.einsum("rh,hc->cr", hidden_two, output_weight, preferred_element_type=jnp.float32)
    slab_values = network.reshape(2, y_count, z_count, SLAB)
    zero = jnp.zeros((), jnp.int32)
    placed = lax.dynamic_update_slice(
        jnp.zeros((2, y_count, z_count, grid), jnp.float32),
        slab_values,
        (zero, zero, zero, first_plane),
    )
    plane_index = jnp.arange(grid, dtype=jnp.int32)
    inside = (plane_index >= first_plane) & (plane_index < first_plane + SLAB)
    fields = jnp.where(inside, placed, fixed_mask.astype(jnp.float32) * background)

    cosine, sine = angles(grid, length, length)
    x_forward = jnp.stack([cosine, -sine], 1).reshape(grid, 2, px_size, kx_count)
    y_forward = complex_table(grid, length, length, -1.0).reshape(
        2, px_size, y_count, 2, py_size, ky_count
    )
    z_forward = complex_table(grid, length, length, -1.0).reshape(2, py_size, z_count, 2, length)
    z_inverse = complex_table(length, grid, length, 1.0).reshape(2, length, 2, py_size, z_count)
    y_inverse = complex_table(length, grid, length, 1.0).reshape(
        2, py_size, ky_count, 2, px_size, y_count
    )
    x_inverse = (
        jnp.stack([cosine.T, -sine.T], 0) * (1.0 / float(length) ** 3)
    ).reshape(2, px_size, kx_count, grid)
    tables = (x_forward, y_forward, z_forward, z_inverse, y_inverse, x_inverse)
    ranks = (px_size, py_size)

    kernel_real = kernel[:, 0]
    kernel_imag = kernel[:, 1]
    predicted = round_trip(fields, kernel_real, kernel_imag, 1.0, tables, ranks)
    residual = (predicted - observed) / grid
    adjoint = round_trip(residual, kernel_real, kernel_imag, -1.0, tables, ranks)
    cotangent = (
        lax.dynamic_slice(adjoint, (zero, zero, zero, first_plane), (2, y_count, z_count, SLAB))
        .reshape(2, -1)
        .astype(jnp.bfloat16)
    )
    grad_output = jnp.einsum("rh,cr->hc", hidden_two, cotangent, preferred_element_type=jnp.float32)
    back_two = jnp.einsum("cr,hc->rh", cotangent, output_weight, preferred_element_type=jnp.float32)
    two_values = hidden_two.astype(jnp.float32)
    delta_two = (back_two * (1.0 - two_values * two_values)).astype(jnp.bfloat16)
    grad_second = jnp.einsum("rh,rk->hk", hidden_one, delta_two, preferred_element_type=jnp.float32)
    back_one = jnp.einsum("rk,hk->rh", delta_two, second_weight, preferred_element_type=jnp.float32)
    one_values = hidden_one.astype(jnp.float32)
    delta_one = (back_one * (1.0 - one_values * one_values)).astype(jnp.bfloat16)
    grad_first = jnp.einsum("rf,rh->fh", features, delta_one, preferred_element_type=jnp.float32)
    grad_first, grad_second, grad_output = gradient_sum((grad_first, grad_second, grad_output))
    return (predicted, grad_first, grad_second, grad_output)


def solution(mesh):
    return jax.shard_map(
        on_device,
        mesh=mesh,
        in_specs=(
            P(),
            P("px", "py", None),
            P(None, "px", "py", None),
            P(None, "px", "py", None),
            P(None, None, "px", "py", None),
            P(),
            P(),
            P(),
            P(),
        ),
        out_specs=(P(None, "px", "py", None), P(), P(), P()),
        check_vma=False,
    )
```

time: 836 us -> 410 us (0.49)
  waiting for transfers between devices: 242 us -> 28.9 us
  starting transfers between devices: 196 us -> 27.9 us
  blocking collectives: 77.7 us -> 121 us
  matrix products: 105 us -> 67.3 us
  local copies, waits for them, and re-layouts: 137 us -> 122 us
  between operations: 17.1 us -> 2.36 us
  other arithmetic: 46.3 us -> 35.2 us
    psum x1 -> x0, waiting for transfers between devices: 175 us -> none  [on_device(): lax.psum((grad_first, grad_second, grad_output), ('px', 'py'))]
    all_to_all x32 -> x4, starting transfers between devices: 196 us -> 27.9 us  [the longest x1 12.3 us: round_trip(): spectrum = lax.all_to_all(spectrum, 'px', 0, 0, tiled=True)]
    all_to_all x0 -> x6, blocking collectives: none -> 121 us  [the longest x1 31.7 us: gradient_sum(): lax.all_to_all(padded.reshape(devices, share), ('px', 'py'), 0, 0, tiled=...]
    psum x1 -> x0, blocking collectives: 77.7 us -> none  [on_device(): lax.psum((grad_first, grad_second, grad_output), ('px', 'py'))]
    all_to_all x32 -> x4, waiting for transfers between devices: 67.8 us -> 28.9 us  [the longest x1 10.4 us: round_trip(): back = lax.all_to_all(back, 'px', 0, 0, tiled=True)]
    dot_general x72 -> x12, matrix products: 93.3 us -> 59.8 us  [contract(): return jnp.einsum(form, values, table, precision=PRECISION)]
    another operation x25 -> x0, local copies, waits for them, and re-layouts: 31.3 us -> none
    all_to_all x32 -> x9, other arithmetic: 40.8 us -> 15.6 us  [the longest x2 3.96 us: round_trip(): back = lax.all_to_all(back, 'px', 0, 0, tiled=True)]
  transfers between devices with their start and end apart: 33 -> 4, of which waited for: 19 -> 4; matrix products, arithmetic and copies ran while one was open for 26% -> 4% of each run, Pallas kernels for 0% -> 0%
where the time goes in v1:
time: 410 us; the launch traced here: 404 us
  local copies, waits for them, and re-layouts  122 us (30%)
  blocking collectives  121 us (30%)
  matrix products  67.3 us (16%)
  other arithmetic  35.2 us (9%)
  waiting for transfers between devices  28.9 us (7%)
  starting transfers between devices  27.9 us (7%)
    dot_general x12, matrix products, contract(): return jnp.einsum(form, values, table, precision=PRECISION)  59.8 us
    unnamed x83, local copies, waits for them, and re-layouts  41.2 us
    all_to_all x1, blocking collectives, gradient_sum(): lax.all_to_all(padded.reshape(devices, share), ('px', 'py'), 0, 0, tiled=...  31.7 us
    all_to_all x1, blocking collectives, gradient_sum(): lax.all_to_all(gathered, ('px', 'py'), 0, 0, tiled=True).reshape(-1)  29.1 us
    transpose x8, local copies, waits for them, and re-layouts, contract(): return jnp.einsum(form, values, table, precision=PRECISION)  23.1 us
    all_to_all x4, local copies, waits for them, and re-layouts, round_trip(): back = lax.all_to_all(back, 'py', 0, 0, tiled=True)  21.7 us
    slice x4, local copies, waits for them, and re-layouts, gradient_sum(): result.append(gathered[offset:offset + part.size].reshape(part.shape))  18.6 us
    all_to_all x1, blocking collectives, round_trip(): back = lax.all_to_all(back, 'px', 0, 0, tiled=True)  15.4 us
  transfers between devices with their start and end apart: 4, of which 4 were waited for; matrix products, arithmetic and copies ran while one was open for 4% of the time, Pallas kernels for 0%

profile of v1, /device:TPU:1, one launch (start us, length us, event | category | flops | bytes accessed | tf_op | source)
XLA Modules:
  0.0 404.2 jit_solution(10218700120018072915)
XLA Ops:
  2.9 3.8 sine_convert_fusion
  6.7 1.5 fusion.9
  11.3 2.5 dynamic_update_slice.3
  15.1 1.5 reshape.622
  16.6 12.3 %all-to-all-start = ((f32[16,1,4096]{2,1,0:T(1,128)}), f32[16,1,4096]{2,1,0:T(1,128)S(1)}, u32[]{:S(2)}, u32[]{:S(2)}) async-start(f32[16,1,4096]{2,1,0:T(1,128)} %reshape.622), calls=%async_computation | async-start | bytes 524288 | tf_op jit(solution)/shard_map/all_to_all | solution.py:34
  28.9 5.6 %broadcast_multiply_fusion = (f32[1,16,8,1,16,16]{1,5,2,0,4,3:T(8,128)}, f32[1,16,8,1,16,16]{1,5,2,0,4,3:T(8,128)}, f32[1,16,8,1,16,16]{1,5,2,0,4,3:T(8,128)}) fusion(s32[16,16]{1,0:T(8,128)S(1)} %multiply_add_fusion, s32[16,8]{0,1:T(8,128)S(1)} %multiply_add_fusion.1), kind=kLoop, calls=%fused_computation.82 | loop fusion | flops 491520 | bytes 394752 | tf_op jit(solution)/shard_map/mul | solution.py:21
  34.5 6.6 %all-to-all-done = f32[16,1,4096]{2,1,0:T(1,128)S(1)} async-done(((f32[16,1,4096]{2,1,0:T(1,128)}), f32[16,1,4096]{2,1,0:T(1,128)S(1)}, u32[]{:S(2)}, u32[]{:S(2)}) %all-to-all-start) | async-done | bytes 262176 | tf_op jit(solution)/shard_map/all_to_all | solution.py:34
  43.6 11.1 %fusion.12 = f32[16,2,2,8,16,16]{4,5,3,2,0,1:T(8,128)} fusion(f32[1,16,8,1,16,16]{1,5,2,0,4,3:T(8,128)} %get-tuple-element.33, f32[1,16,8,1,16,16]{1,5,2,0,4,3:T(8,128)} %get-tuple-element.32, f32[1,16,8,1,16,16]{1,5,2,0,4,3:T(8,128)} %get-tuple-element.31, f32[16,2,2,8,8,16,1,1]{5,4,3,2,1,0,7,6:T(8,128)S(1)} %bitcast.232), kind=kOutput, calls=%fused_computation.19 | convolution fusion | flops 201719808 | bytes 1179648 | tf_op jit(solution)/shard_map/scfyzl,csydmq->mdfzlq/dot_general | solution.py:27
  54.8 5.6 %copy.92 = f32[16,2,2,8,16,16]{5,3,1,4,2,0:T(8,128)} copy(f32[16,2,2,8,16,16]{4,5,3,2,0,1:T(8,128)} %fusion.12) | data formatting | bytes 1048576 | tf_op jit(solution)/shard_map/scfyzl,csydmq->mdfzlq/transpose | solution.py:27
  60.3 4.2 %reshape.624 = f32[16,1,8192]{2,1,0:T(1,128)} reshape(f32[16,2,16,2,8,16]{5,4,3,2,1,0:T(8,128)} %bitcast.225) | data formatting | bytes 1048576
  64.5 6.7 %all-to-all-start.1 = ((f32[16,1,8192]{2,1,0:T(1,128)}), f32[16,1,8192]{2,1,0:T(1,128)S(1)}, u32[]{:S(2)}, u32[]{:S(2)}) async-start(f32[16,1,8192]{2,1,0:T(1,128)} %reshape.624), calls=%async_computation.1 | async-start | bytes 1048576 | tf_op jit(solution)/shard_map/all_to_all | solution.py:36
  72.6 8.2 %all-to-all-done.1 = f32[16,1,8192]{2,1,0:T(1,128)S(1)} async-done(((f32[16,1,8192]{2,1,0:T(1,128)}), f32[16,1,8192]{2,1,0:T(1,128)S(1)}, u32[]{:S(2)}, u32[]{:S(2)}) %all-to-all-start.1) | async-done | bytes 524320 | tf_op jit(solution)/shard_map/all_to_all | solution.py:36
  80.8 1.9 reduce.4
  82.7 2.8 reshape.625
  85.5 5.8 %copy.93 = f32[16,2,2,8,16,16]{0,5,3,1,4,2:T(8,128)} copy(f32[16,2,2,8,16,16]{5,3,1,4,2,0:T(8,128)} %bitcast.226) | data formatting | bytes 1048576 | tf_op jit(solution)/shard_map/all_to_all | solution.py:36
  91.3 4.9 %fusion.23 = f32[2,2,16,16,256]{4,3,2,1,0:T(8,128)S(1)} fusion(f32[16,2,2,8,16,16]{0,5,3,1,4,2:T(8,128)} %copy.93, f32[1,16,8,1,256]{4,1,2,0,3:T(8,128)S(1)} %get-tuple-element.41, f32[1,16,8,1,256]{4,1,2,0,3:T(8,128)S(1)} %get-tuple-element.40, f32[1,16,8,1,256]{4,1,2,0,3:T(8,128)S(1)} %get-tuple-element.39), kind=kOutput, calls=%fused_computation.44 | convolution fusion | flops 403046400 | bytes 1966080 | tf_op jit(solution)/shard_map/sdfzlq,dszek->eflqk/dot_general | solution.py:27
  96.5 3.5 convolution_bitcast_fusion.2
  100.0 2.7 copy.183
  102.7 4.2 %reshape.626 = f32[16,1,8192]{2,1,0:T(1,128)} reshape(f32[16,2,8,2,16,16]{5,4,3,2,1,0:T(8,128)} %bitcast.227) | data formatting | bytes 1048576
  106.9 4.9 %all-to-all-start.2 = ((f32[16,1,8192]{2,1,0:T(1,128)}), f32[16,1,8192]{2,1,0:T(1,128)S(1)}, u32[]{:S(2)}, u32[]{:S(2)}) async-start(f32[16,1,8192]{2,1,0:T(1,128)} %reshape.626), calls=%async_computation.2 | async-start | bytes 1048576 | tf_op jit(solution)/shard_map/all_to_all | solution.py:44
  111.9 6.0 %fusion.53 = (f32[1,16,16,1,16,8]{4,1,2,0,3,5:T(8,128)S(1)}, f32[1,16,16,1,16,8]{4,1,2,0,3,5:T(8,128)}, f32[1,16,16,1,16,8]{4,1,2,0,3,5:T(8,128)}) fusion(s32[16,8]{0,1:T(8,128)S(1)} %multiply_add_fusion.1, s32[16,16]{0,1:T(8,128)S(1)} %copy.87), kind=kLoop, calls=%fused_computation.86 | loop fusion | flops 491520 | bytes 394752 | tf_op jit(solution)/shard_map/sin | solution.py:16
  117.8 3.6 all-to-all-done.2
  121.5 1.9 reduce.5
  123.4 2.8 reshape.627
  126.2 4.9 %bitcast_bitcast_fusion.1 = f32[16,2,2,16,16,8,1,1]{4,3,2,5,1,0,7,6:T(8,128)} fusion(f32[16,2,8,2,16,16]{5,4,3,2,1,0:T(8,128)} %reshape.627), kind=kLoop, calls=%fused_computation.179 | loop fusion | bytes 1048576 | tf_op jit(solution)/shard_map/all_to_all | solution.py:44
  131.1 5.9 %copy.125 = f32[16,2,2,16,16,8,1,1]{0,5,4,1,3,6,7,2:T(8,128)} copy(f32[16,2,2,16,16,8,1,1]{4,3,2,5,1,0,7,6:T(8,128)} %bitcast_bitcast_fusion.1) | data formatting | bytes 1048576 | tf_op jit(solution)/shard_map/all_to_all | solution.py:44
  137.0 8.1 %fusion.20 = f32[16,2,2,8,8,16]{0,4,5,1,3,2:T(8,128)} fusion(f32[16,2,2,16,16,8,1,1]{0,5,4,1,3,6,7,2:T(8,128)} %copy.125, f32[1,16,16,1,16,8]{4,1,2,0,3,5:T(8,128)} %get-tuple-element.30, f32[1,16,16,1,16,8]{4,1,2,0,3,5:T(8,128)S(1)} %copy-done.10, f32[1,16,16,1,16,8]{4,1,2,0,3,5:T(8,128)S(1)} %get-tuple-element.28), kind=kOutput, calls=%fused_computation.35 | convolution fusion | flops 201719808 | bytes 1179648 | tf_op jit(solution)/shard_map/sgflqz,gsqhmy->mhfyzl/dot_general | solution.py:27
  145.1 3.0 copy.99
  148.1 1.5 reshape.628
  149.6 3.9 all-to-all-start.3
  154.8 10.4 %all-to-all-done.3 = f32[16,1,4096]{2,1,0:T(1,128)S(1)} async-done(((f32[16,1,4096]{2,1,0:T(1,128)}), f32[16,1,4096]{2,1,0:T(1,128)S(1)}, u32[]{:S(2)}, u32[]{:S(2)}) %all-to-all-start.3) | async-done | bytes 262176 | tf_op jit(solution)/shard_map/all_to_all | solution.py:46
  165.2 2.0 reduce.6
  167.2 1.7 reshape.629
  168.8 2.0 fusion.30
  171.4 1.9 convolution_bitcast_fusion.3
  174.4 15.4 %all_to_all.56 = f32[16,1,4096]{2,1,0:T(1,128)S(1)} all-to-all(f32[16,1,4096]{2,1,0:T(1,128)S(1)} %reshape.630), channel_id=1, replica_groups=mesh['px'=16,'py'=16] {'px'}, dimensions={0} | all-to-all | bytes 524288 | tf_op jit(solution)/shard_map/all_to_all | solution.py:34
  191.8 11.1 %fusion.13 = f32[16,2,2,8,16,16]{4,5,3,2,0,1:T(8,128)} fusion(f32[1,16,8,1,16,16]{1,5,2,0,4,3:T(8,128)} %get-tuple-element.33, f32[1,16,8,1,16,16]{1,5,2,0,4,3:T(8,128)} %get-tuple-element.32, f32[1,16,8,1,16,16]{1,5,2,0,4,3:T(8,128)} %get-tuple-element.31, f32[16,2,2,8,8,16,1,1]{5,4,3,2,1,0,7,6:T(8,128)S(1)} %bitcast.231), kind=kOutput, calls=%fused_computation.20 | convolution fusion | flops 201719808 | bytes 1179648 | tf_op jit(solution)/shard_map/scfyzl,csydmq->mdfzlq/dot_general | solution.py:27
  202.9 5.6 %copy.103 = f32[16,2,2,8,16,16]{5,3,1,4,2,0:T(8,128)} copy(f32[16,2,2,8,16,16]{4,5,3,2,0,1:T(8,128)} %fusion.13) | data formatting | bytes 1048576 | tf_op jit(solution)/shard_map/scfyzl,csydmq->mdfzlq/transpose | solution.py:27
  208.6 3.5 reshape.632
  212.1 15.4 %all_to_all.57 = f32[16,1,8192]{2,1,0:T(1,128)S(1)} all-to-all(f32[16,1,8192]{2,1,0:T(1,128)S(1)} %reshape.632), channel_id=1, replica_groups=mesh['px'=16,'py'=16] {'py'}, dimensions={0} | all-to-all | bytes 1048576 | tf_op jit(solution)/shard_map/all_to_all | solution.py:36
  227.4 1.9 reduce.8
  229.3 2.8 reshape.633
  232.2 5.8 %copy.104 = f32[16,2,2,8,16,16]{0,5,3,1,4,2:T(8,128)} copy(f32[16,2,2,8,16,16]{5,3,1,4,2,0:T(8,128)} %bitcast.229) | data formatting | bytes 1048576 | tf_op jit(solution)/shard_map/all_to_all | solution.py:36
  238.1 4.9 %fusion.26 = f32[2,2,16,16,256]{4,3,2,1,0:T(8,128)S(1)} fusion(f32[16,2,2,8,16,16]{0,5,3,1,4,2:T(8,128)} %copy.104, f32[1,16,8,1,256]{4,1,2,0,3:T(8,128)S(1)} %copy-done.28, f32[1,16,8,1,256]{4,1,2,0,3:T(8,128)S(1)} %copy-done.26, f32[1,16,8,1,256]{4,1,2,0,3:T(8,128)S(1)} %copy-done.24), kind=kOutput, calls=%fused_computation.45 | convolution fusion | flops 403046400 | bytes 1966080 | tf_op jit(solution)/shard_map/sdfzlq,dszek->eflqk/dot_general | solution.py:27
  243.2 3.5 convolution_bitcast_fusion.1
  246.7 2.7 copy.182
  249.4 3.5 reshape.634
  252.9 13.7 %all_to_all.58 = f32[16,1,8192]{2,1,0:T(1,128)S(1)} all-to-all(f32[16,1,8192]{2,1,0:T(1,128)S(1)} %reshape.634), channel_id=1, replica_groups=mesh['px'=16,'py'=16] {'py'}, dimensions={0} | all-to-all | bytes 1048576 | tf_op jit(solution)/shard_map/all_to_all | solution.py:44
  266.6 1.9 reduce.9
  268.4 2.8 reshape.635
  271.3 4.9 %bitcast_bitcast_fusion = f32[16,2,2,16,16,8,1,1]{4,3,2,5,1,0,7,6:T(8,128)} fusion(f32[16,2,8,2,16,16]{5,4,3,2,1,0:T(8,128)} %reshape.635), kind=kLoop, calls=%fused_computation.178 | loop fusion | bytes 1048576 | tf_op jit(solution)/shard_map/all_to_all | solution.py:44
  276.2 6.0 %copy.136 = f32[16,2,2,16,16,8,1,1]{0,5,4,1,3,6,7,2:T(8,128)} copy(f32[16,2,2,16,16,8,1,1]{4,3,2,5,1,0,7,6:T(8,128)} %bitcast_bitcast_fusion) | data formatting | bytes 1048576 | tf_op jit(solution)/shard_map/all_to_all | solution.py:44
  282.2 6.8 %fusion.21 = f32[16,2,2,8,8,16]{0,4,5,1,3,2:T(8,128)} fusion(f32[16,2,2,16,16,8,1,1]{0,5,4,1,3,6,7,2:T(8,128)} %copy.136, f32[1,16,16,1,16,8]{4,1,2,0,3,5:T(8,128)S(1)} %copy-done.12, f32[1,16,16,1,16,8]{4,1,2,0,3,5:T(8,128)S(1)} %copy-done.11, f32[1,16,16,1,16,8]{4,1,2,0,3,5:T(8,128)S(1)} %copy-done.9), kind=kOutput, calls=%fused_computation.36 | convolution fusion | flops 201719808 | bytes 1179648 | tf_op jit(solution)/shard_map/sgflqz,gsqhmy->mhfyzl/dot_general | solution.py:27
  289.0 3.1 copy.109
  292.1 1.5 reshape.636
  293.5 15.4 %all_to_all.59 = f32[16,1,4096]{2,1,0:T(1,128)S(1)} all-to-all(f32[16,1,4096]{2,1,0:T(1,128)} %reshape.636), channel_id=1, replica_groups=mesh['px'=16,'py'=16] {'px'}, dimensions={0} | all-to-all | bytes 524288 | tf_op jit(solution)/shard_map/all_to_all | solution.py:46
  309.0 2.0 reduce.10
  311.0 1.7 reshape.637
  315.4 2.4 fusion.29
  317.9 1.7 convolution_bitcast_fusion.5
  321.4 31.7 %all_to_all.60 = f32[256,1,514]{2,1,0:T(1,128)S(1)} all-to-all(f32[256,1,514]{2,1,0:T(1,128)S(1)} %all_to_all.45), channel_id=1, replica_groups=mesh['px'=16,'py'=16] {'px','py'}, dimensions={0} | all-to-all | bytes 1052672 | tf_op jit(solution)/shard_map/all_to_all | solution.py:56
  354.0 29.1 %all_to_all.61 = f32[256,1,514]{2,1,0:T(1,128)S(1)} all-to-all(f32[256,1,514]{2,1,0:T(1,128)S(1)} %broadcast_in_dim.10), channel_id=1, replica_groups=mesh['px'=16,'py'=16] {'px','py'}, dimensions={0} | all-to-all | bytes 1052672 | tf_op jit(solution)/shard_map/all_to_all | solution.py:59
  383.1 1.6 reduce.1
  384.6 16.2 %slice.58 = f32[65792,2]{1,0:T(8,128)} reshape(f32[256,514]{1,0:T(8,128)S(1)} %reduce.1) | data formatting | bytes 1052672 | tf_op jit(solution)/shard_map/slice | solution.py:63
  (112 shorter events, 23.6 us)
Async XLA Ops:
  0.6 8.6 %copy-start = (bf16[256,256]{1,0:T(8,128)(2,1)S(1)}, bf16[256,256]{1,0:T(8,128)(2,1)}, u32[]{:S(2)}) copy-start(bf16[256,256]{1,0:T(8,128)(2,1)} %param.16) | copy-start | bytes 393220
  0.6 10.1 %copy-start.31 = (bf16[256,2]{0,1:T(2,128)(2,1)S(1)}, bf16[256,2]{0,1:T(2,128)(2,1)}, u32[]{:S(2)}) copy-start(bf16[256,2]{0,1:T(2,128)(2,1)} %param.17) | copy-start | bytes 3076
  0.7 10.6 %copy-start.30 = (s32[8,8,128]{2,1,0:T(8,128)S(1)}, s32[8,8,128]{2,1,0:T(8,128)}, u32[]{:S(2)}) copy-start(s32[8,8,128]{2,1,0:T(8,128)} %param.10) | copy-start | bytes 98308
  0.7 13.1 %copy-start.29 = (f32[2,8,8,128]{3,2,1,0:T(8,128)S(1)}, f32[2,8,8,128]{3,2,1,0:T(8,128)}, u32[]{:S(2)}) copy-start(f32[2,8,8,128]{3,2,1,0:T(8,128)} %param.11) | copy-start | bytes 196612
  6.7 3.0 copy-start.14
  6.7 3.0 copy-start.15
  8.2 1.1 copy-start.4
  9.7 1.0 copy-start.2
  16.6 24.6 %all-to-all-start = ((f32[16,1,4096]{2,1,0:T(1,128)}), f32[16,1,4096]{2,1,0:T(1,128)S(1)}, u32[]{:S(2)}, u32[]{:S(2)}) async-start(f32[16,1,4096]{2,1,0:T(1,128)} %reshape.622), calls=%async_computation | async-start | bytes 524288 | tf_op jit(solution)/shard_map/all_to_all | solution.py:34
  64.5 16.3 %all-to-all-start.1 = ((f32[16,1,8192]{2,1,0:T(1,128)}), f32[16,1,8192]{2,1,0:T(1,128)S(1)}, u32[]{:S(2)}, u32[]{:S(2)}) async-start(f32[16,1,8192]{2,1,0:T(1,128)} %reshape.624), calls=%async_computation.1 | async-start | bytes 1048576 | tf_op jit(solution)/shard_map/all_to_all | solution.py:36
  71.9 19.4 %copy-start.23 = (f32[1,16,8,1,256]{4,1,2,0,3:T(8,128)}, f32[1,16,8,1,256]{4,1,2,0,3:T(8,128)S(1)}, u32[]{:S(2)}) copy-start(f32[1,16,8,1,256]{4,1,2,0,3:T(8,128)S(1)} %get-tuple-element.39) | copy-start | bytes 393220
  71.9 19.4 %copy-start.25 = (f32[1,16,8,1,256]{4,1,2,0,3:T(8,128)}, f32[1,16,8,1,256]{4,1,2,0,3:T(8,128)S(1)}, u32[]{:S(2)}) copy-start(f32[1,16,8,1,256]{4,1,2,0,3:T(8,128)S(1)} %get-tuple-element.40) | copy-start | bytes 393220
  71.9 19.4 %copy-start.27 = (f32[1,16,8,1,256]{4,1,2,0,3:T(8,128)}, f32[1,16,8,1,256]{4,1,2,0,3:T(8,128)S(1)}, u32[]{:S(2)}) copy-start(f32[1,16,8,1,256]{4,1,2,0,3:T(8,128)S(1)} %get-tuple-element.41) | copy-start | bytes 393220
  72.5 24.0 %copy-start.17 = (f32[1,256,1,16,8]{1,4,3,2,0:T(8,128)}, f32[1,256,1,16,8]{1,4,3,2,0:T(8,128)S(1)}, u32[]{:S(2)}) copy-start(f32[1,256,1,16,8]{1,4,3,2,0:T(8,128)S(1)} %get-tuple-element.36) | copy-start | bytes 393220
  72.6 24.0 %copy-start.19 = (f32[1,256,1,16,8]{1,4,3,2,0:T(8,128)}, f32[1,256,1,16,8]{1,4,3,2,0:T(8,128)S(1)}, u32[]{:S(2)}) copy-start(f32[1,256,1,16,8]{1,4,3,2,0:T(8,128)S(1)} %get-tuple-element.37) | copy-start | bytes 393220
  72.6 24.0 %copy-start.21 = (f32[1,256,1,16,8]{1,4,3,2,0:T(8,128)}, f32[1,256,1,16,8]{1,4,3,2,0:T(8,128)S(1)}, u32[]{:S(2)}) copy-start(f32[1,256,1,16,8]{1,4,3,2,0:T(8,128)S(1)} %get-tuple-element.38) | copy-start | bytes 393220
  91.3 5.0 %copy-start.1 = (f32[2,2,16,16,256]{4,3,2,1,0:T(8,128)S(1)}, f32[2,2,16,16,256]{4,3,2,1,0:T(8,128)}, u32[]{:S(2)}) copy-start(f32[2,2,16,16,256]{4,3,2,1,0:T(8,128)} %param.13) | copy-start | bytes 3145732
  106.9 14.6 %all-to-all-start.2 = ((f32[16,1,8192]{2,1,0:T(1,128)}), f32[16,1,8192]{2,1,0:T(1,128)S(1)}, u32[]{:S(2)}, u32[]{:S(2)}) async-start(f32[16,1,8192]{2,1,0:T(1,128)} %reshape.626), calls=%async_computation.2 | async-start | bytes 1048576 | tf_op jit(solution)/shard_map/all_to_all | solution.py:44
  117.8 19.2 %copy-start.8 = (f32[1,16,16,1,16,8]{4,1,2,0,3,5:T(8,128)}, f32[1,16,16,1,16,8]{4,1,2,0,3,5:T(8,128)S(1)}, u32[]{:S(2)}) copy-start(f32[1,16,16,1,16,8]{4,1,2,0,3,5:T(8,128)S(1)} %get-tuple-element.28) | copy-start | bytes 393220
  131.1 5.9 %copy-start.10 = (f32[1,16,16,1,16,8]{4,1,2,0,3,5:T(8,128)S(1)}, f32[1,16,16,1,16,8]{4,1,2,0,3,5:T(8,128)}, u32[]{:S(2)}) copy-start(f32[1,16,16,1,16,8]{4,1,2,0,3,5:T(8,128)} %get-tuple-element.29) | copy-start | bytes 393220
  149.6 15.6 %all-to-all-start.3 = ((f32[16,1,4096]{2,1,0:T(1,128)}), f32[16,1,4096]{2,1,0:T(1,128)S(1)}, u32[]{:S(2)}, u32[]{:S(2)}) async-start(f32[16,1,4096]{2,1,0:T(1,128)} %reshape.628), calls=%async_computation.3 | async-start | bytes 524288 | tf_op jit(solution)/shard_map/all_to_all | solution.py:46
  170.8 0.6 copy-start.16
  232.2 5.9 %copy-start.24 = (f32[1,16,8,1,256]{4,1,2,0,3:T(8,128)S(1)}, f32[1,16,8,1,256]{4,1,2,0,3:T(8,128)}, u32[]{:S(2)}) copy-start(f32[1,16,8,1,256]{4,1,2,0,3:T(8,128)} %copy-done.23) | copy-start | bytes 393220
  232.2 5.9 %copy-start.26 = (f32[1,16,8,1,256]{4,1,2,0,3:T(8,128)S(1)}, f32[1,16,8,1,256]{4,1,2,0,3:T(8,128)}, u32[]{:S(2)}) copy-start(f32[1,16,8,1,256]{4,1,2,0,3:T(8,128)} %copy-done.25) | copy-start | bytes 393220
  232.2 5.9 %copy-start.28 = (f32[1,16,8,1,256]{4,1,2,0,3:T(8,128)S(1)}, f32[1,16,8,1,256]{4,1,2,0,3:T(8,128)}, u32[]{:S(2)}) copy-start(f32[1,16,8,1,256]{4,1,2,0,3:T(8,128)} %copy-done.27) | copy-start | bytes 393220
  238.0 5.2 %copy-start.18 = (f32[1,256,1,16,8]{1,4,3,2,0:T(8,128)S(1)}, f32[1,256,1,16,8]{1,4,3,2,0:T(8,128)}, u32[]{:S(2)}) copy-start(f32[1,256,1,16,8]{1,4,3,2,0:T(8,128)} %copy-done.17) | copy-start | bytes 393220
  238.0 5.2 %copy-start.20 = (f32[1,256,1,16,8]{1,4,3,2,0:T(8,128)S(1)}, f32[1,256,1,16,8]{1,4,3,2,0:T(8,128)}, u32[]{:S(2)}) copy-start(f32[1,256,1,16,8]{1,4,3,2,0:T(8,128)} %copy-done.19) | copy-start | bytes 393220
  238.0 5.2 %copy-start.22 = (f32[1,256,1,16,8]{1,4,3,2,0:T(8,128)S(1)}, f32[1,256,1,16,8]{1,4,3,2,0:T(8,128)}, u32[]{:S(2)}) copy-start(f32[1,256,1,16,8]{1,4,3,2,0:T(8,128)} %copy-done.21) | copy-start | bytes 393220
  276.2 6.0 %copy-start.9 = (f32[1,16,16,1,16,8]{4,1,2,0,3,5:T(8,128)S(1)}, f32[1,16,16,1,16,8]{4,1,2,0,3,5:T(8,128)}, u32[]{:S(2)}) copy-start(f32[1,16,16,1,16,8]{4,1,2,0,3,5:T(8,128)} %copy-done.8) | copy-start | bytes 393220
  276.2 6.0 %copy-start.11 = (f32[1,16,16,1,16,8]{4,1,2,0,3,5:T(8,128)S(1)}, f32[1,16,16,1,16,8]{4,1,2,0,3,5:T(8,128)}, u32[]{:S(2)}) copy-start(f32[1,16,16,1,16,8]{4,1,2,0,3,5:T(8,128)} %get-tuple-element.29) | copy-start | bytes 393220
  276.2 6.0 %copy-start.12 = (f32[1,16,16,1,16,8]{4,1,2,0,3,5:T(8,128)S(1)}, f32[1,16,16,1,16,8]{4,1,2,0,3,5:T(8,128)}, u32[]{:S(2)}) copy-start(f32[1,16,16,1,16,8]{4,1,2,0,3,5:T(8,128)} %get-tuple-element.30) | copy-start | bytes 393220
  289.0 23.7 %copy-start.6 = (f32[1,16,16,128]{3,2,1,0:T(8,128)S(1)}, f32[1,16,16,128]{3,2,1,0:T(8,128)}, u32[]{:S(2)}) copy-start(f32[1,16,16,128]{3,2,1,0:T(8,128)} %get-tuple-element.34) | copy-start | bytes 393220
  289.0 23.7 %copy-start.7 = (f32[1,16,16,128]{3,2,1,0:T(8,128)S(1)}, f32[1,16,16,128]{3,2,1,0:T(8,128)}, u32[]{:S(2)}) copy-start(f32[1,16,16,128]{3,2,1,0:T(8,128)} %get-tuple-element.35) | copy-start | bytes 393220
  292.1 21.8 %copy-start.3 = (bf16[2048,256]{1,0:T(8,128)(2,1)S(1)}, bf16[2048,256]{1,0:T(8,128)(2,1)}, u32[]{:S(2)}) copy-start(bf16[2048,256]{1,0:T(8,128)(2,1)} %copy-done.2) | copy-start | bytes 3145732
  313.8 4.0 copy-start.5
  314.4 1.0 copy-start.13
